TPU v7x, 32 devices: a whole 2x2x4 slice. The times are simulated.
32 devices in a mesh: row: 4 (over y, core), col: 8 (over z, x).
Axes of the slice: x: 2, y: 2, z: 4, core: 2. Of those that a mesh axis runs over, the one named last changes fastest.
Arguments:
- factor: float32 [6, 2048, 6, 2048], P(None, 'row', None, 'col'), may hold values from -0.0625 to 0.0625
- diag_inv: float32 [6, 2048, 2048], P(None, None, 'row'), may hold values from -2 to 2, as said below
- structure: int32 [6, 6, 16], P(None, None, 'row'), may hold values 0 or 1
- parent: int32 [6], replicated, may hold values from 1 to 6, as said below
- post: float32 [6, 2048, 64], P(None, 'row', 'col'), may hold values from -6 to 6
Outputs:
- mean_x: float32 [6, 2048, 64], P(None, 'row', 'col')
- variance: float32 [6, 2048], P(None, 'row')
Inputs may be any that keep to these rules, and one draw needn't show every extreme that they name: parent[s] > s for s < 5, and parent[5] = 6; every supernode has at most 2 ancestors, and some supernode has exactly that many. The diagonal of each diag_inv[s] lies in 0.5 to 2.
All inputs are finite; a program needn't handle non-finite values. No bound on the sum of `structure` on one device may be relied on, other than what follows from the above.
Results may differ from a plain program's by a relative error of at most 0.00014.
Values sent between devices are 32-bit elements; how exact they have to be, the bound alone decides.
A program may use at most 192 MiB of HBM per device.

v0:
```python
import jax
import jax.numpy as jnp
from jax import lax
from jax.sharding import PartitionSpec as P

HIGH = lax.Precision.HIGH


def product(left, right):
    return jnp.dot(left, right, precision=HIGH, preferred_element_type=jnp.float32)


def body(factor, diag_inv, structure, parent, post):
    super_count = factor.shape[0]
    row_width = factor.shape[1]
    col_width = factor.shape[3]
    full_width = diag_inv.shape[1]
    row_at = lax.axis_index("row")
    col_at = lax.axis_index("col")
    last = super_count - 1
    block_rows = row_width // structure.shape[2]
    extended = jnp.concatenate([parent, jnp.full((1,), super_count, jnp.int32)])
    first_at = parent
    second_at = extended[parent]

    def pick(current_sup, target):
        clamped = jnp.minimum(target, last)
        block = lax.dynamic_index_in_dim(factor[:, :, current_sup, :], clamped, 0, keepdims=False)
        flags = lax.dynamic_index_in_dim(structure[current_sup], clamped, 0, keepdims=False)
        flags = jnp.where(target < super_count, flags.astype(jnp.float32), 0.0)
        return block * jnp.repeat(flags, block_rows)[:, None]

    blocks = [None] * super_count
    for current_sup in range(last - 1, -1, -1):
        mine = jnp.concatenate(
            [pick(current_sup, first_at[current_sup]), pick(current_sup, second_at[current_sup])],
            axis=0,
        )
        blocks[current_sup] = lax.all_gather(mine, "col", axis=1, tiled=True)
    own_cols = row_at * row_width + jnp.arange(row_width, dtype=jnp.int32)
    rows_full = jnp.arange(full_width, dtype=jnp.int32)
    keep = rows_full[:, None] >= own_cols[None, :]
    lower = [jnp.where(keep, diag_inv[s], 0.0) for s in range(super_count)]
    unit_rows = col_at * col_width + jnp.arange(col_width, dtype=jnp.int32)
    own = lax.dynamic_slice_in_dim(diag_inv, col_at * col_width, col_width, axis=1)
    own = jnp.where((unit_rows[:, None] >= own_cols[None, :])[None], own, 0.0)
    gathered = jnp.swapaxes(lax.all_gather(post, "row", axis=1, tiled=True), 1, 2)

    def take(stacked, target):
        return lax.dynamic_index_in_dim(stacked, jnp.minimum(target, last), 0, keepdims=False)

    rhs = jnp.stack([product(gathered[s], lower[s]) for s in range(super_count)])

    def solve(current_sup, unit_part, rhs_part):
        summed = lax.psum(jnp.concatenate([unit_part, rhs_part], axis=0), "row")
        right = jnp.concatenate(
            [-summed[:col_width], gathered[current_sup] - summed[col_width:]], axis=0
        )
        fresh = product(right, lower[current_sup])
        return (fresh[:col_width], fresh[col_width:])

    near = [jnp.zeros((col_width, row_width), jnp.float32)] * super_count
    means = [rhs[s] for s in range(super_count)]
    for s in range(last - 1, -1, -1):
        one, two = (first_at[s], second_at[s])
        unit_part = product(take(own, one), blocks[s][:row_width])
        rhs_part = product(jnp.concatenate([take(rhs, one), take(rhs, two)], axis=1), blocks[s])
        near[s], means[s] = solve(s, unit_part, rhs_part)
    near_all = jnp.stack(near)
    rhs = jnp.stack(means)
    far = [None] * super_count
    for s in range(last - 1, -1, -1):
        one, two = (first_at[s], second_at[s])
        selected = jnp.concatenate(
            [
                jnp.concatenate([take(near_all, one), take(own, two)], axis=1),
                jnp.concatenate([take(rhs, one), take(rhs, two)], axis=1),
            ],
            axis=0,
        )
        both = product(selected, blocks[s])
        far[s], means[s] = solve(s, both[:col_width], both[col_width:])
    squares = []
    for s in range(super_count):
        total = jnp.sum(own[s] * own[s], axis=0)
        if s < last:
            total = total + jnp.sum(near[s] * near[s], axis=0) + jnp.sum(far[s] * far[s], axis=0)
        squares.append(total)
    variance = lax.psum(jnp.stack(squares), "col")
    mean_x = jnp.swapaxes(jnp.stack(means), 1, 2)
    return (mean_x, variance)


def solution(mesh):
    return jax.shard_map(
        body,
        mesh=mesh,
        in_specs=(
            P(None, "row", None, "col"),
            P(None, None, "row"),
            P(None, None, "row"),
            P(),
            P(None, "row", "col"),
        ),
        out_specs=(P(None, "row", "col"), P(None, "row")),
        check_vma=False,
    )
```

profile of v0, /device:TPU:0, one launch (start us, length us, event | category | flops | bytes accessed | tf_op | source)
XLA Modules:
  0.0 1189.7 jit_solution(15968273963925713293)
XLA Ops:
  17.9 11.0 fusion.291
  51.5 8.9 all_gather.19
  84.9 75.8 %all-gather.8.cloned.1.call-done = f32[1024,2048]{1,0:T(8,128)} async-done(((f32[1024,256]{1,0:T(8,128)}), f32[1024,2048]{1,0:T(8,128)}) %all-gather.8.cloned.1.call-update) | async-done | bytes 8388624 | tf_op jit(solution)/shard_map/all_gather | solution.py:39
  165.0 5.9 fusion.204
  172.4 113.5 %all-gather.10.cloned.1.call-done = f32[1024,2048]{1,0:T(8,128)} async-done(((f32[1024,256]{1,0:T(8,128)}), f32[1024,2048]{1,0:T(8,128)}) %all-gather.10.cloned.1.call-update) | async-done | bytes 8388624 | tf_op jit(solution)/shard_map/all_gather | solution.py:39
  290.2 5.7 fusion.208
  297.4 113.8 %all-gather.12.cloned.1.call-done = f32[1024,2048]{1,0:T(8,128)} async-done(((f32[1024,256]{1,0:T(8,128)}), f32[1024,2048]{1,0:T(8,128)}) %all-gather.12.cloned.1.call-update) | async-done | bytes 8388624 | tf_op jit(solution)/shard_map/all_gather | solution.py:39
  415.4 5.7 fusion.212
  422.6 113.6 %all-gather.14.cloned.1.call-done = f32[1024,2048]{1,0:T(8,128)} async-done(((f32[1024,256]{1,0:T(8,128)}), f32[1024,2048]{1,0:T(8,128)}) %all-gather.14.cloned.1.call-update) | async-done | bytes 8388624 | tf_op jit(solution)/shard_map/all_gather | solution.py:39
  540.4 6.1 fusion.216
  548.1 113.2 %all-gather.6.cloned.1.call-done = f32[1024,2048]{1,0:T(8,128)} async-done(((f32[1024,256]{1,0:T(8,128)}), f32[1024,2048]{1,0:T(8,128)}) %all-gather.6.cloned.1.call-update) | async-done | bytes 8388624 | tf_op jit(solution)/shard_map/all_gather | solution.py:39
  665.5 5.5 fusion.200
  675.0 188.1 %all-reduce.7.cloned.1.call-done = (f32[264,2048]{1,0:T(8,128)}, f32[264,2048]{1,0:T(8,128)}, f32[264,2048]{1,0:T(8,128)}, f32[264,2048]{1,0:T(8,128)}, f32[264,2048]{1,0:T(8,128)}) async-done(((f32[264,2048]{1,0:T(8,128)}, f32[264,2048]{1,0:T(8,128)}, f32[264,2048]{1,0:T(8,128)}, f32[264,2048]{1,0:T(8,128)}, f32[264,2048]{1,0:T(8,128)}), (f32[264,2048]{1,0:T(8,128)}, f32[264,2048]{1,0:T(8,128)}, ...) | async-done | bytes 10813456 | tf_op jit(solution)/shard_map/psum | solution.py:55
  887.0 4.4 fusion.43
  893.8 6.0 fusion.139
  899.9 5.8 fusion.147
  905.8 5.8 fusion.155
  911.6 6.1 fusion.163
  917.7 5.8 fusion.171
  923.9 192.1 %all-reduce.5.cloned.1.call-done = (f32[264,2048]{1,0:T(8,128)}, f32[264,2048]{1,0:T(8,128)}, f32[264,2048]{1,0:T(8,128)}, f32[264,2048]{1,0:T(8,128)}, f32[264,2048]{1,0:T(8,128)}) async-done(((f32[264,2048]{1,0:T(8,128)}, f32[264,2048]{1,0:T(8,128)}, f32[264,2048]{1,0:T(8,128)}, f32[264,2048]{1,0:T(8,128)}, f32[264,2048]{1,0:T(8,128)}), (f32[264,2048]{1,0:T(8,128)}, f32[264,2048]{1,0:T(8,128)}, ...) | async-done | bytes 10813456 | tf_op jit(solution)/shard_map/psum | solution.py:55
  1127.0 4.5 fusion.42
  1135.9 4.3 fusion.38
  1140.3 4.3 fusion.36
  1144.9 37.7 %psum.87 = f32[6,512]{1,0:T(8,128)} all-reduce(f32[6,512]{1,0:T(8,128)S(1)} %stack.112), channel_id=1, replica_groups=mesh['row'=4,'col'=8] {'col'}, use_global_device_ids=true, to_apply=%region_26.27 | all-reduce | flops 3072 | bytes 24576 | tf_op jit(solution)/shard_map/psum | solution.py:89
  (208 shorter events, 118.2 us)
Async XLA Ops:
  7.2 153.6 %all-gather.8.cloned.1.call-start = ((), (), s32[]{:S(2)}) async-start(), calls=%async_computation.1 | async-start | bytes 9437184 | tf_op jit(solution)/shard_map/all_gather | solution.py:39
  32.8 253.2 %all-gather.10.cloned.1.call-start = ((), (), s32[]{:S(2)}) async-start(), calls=%async_computation.2 | async-start | bytes 9437184 | tf_op jit(solution)/shard_map/all_gather | solution.py:39
  35.1 376.1 %all-gather.12.cloned.1.call-start = ((), (), s32[]{:S(2)}) async-start(), calls=%async_computation.3 | async-start | bytes 9437184 | tf_op jit(solution)/shard_map/all_gather | solution.py:39
  45.1 491.1 %all-gather.14.cloned.1.call-start = ((), (), s32[]{:S(2)}) async-start(), calls=%async_computation.4 | async-start | bytes 9437184 | tf_op jit(solution)/shard_map/all_gather | solution.py:39
  47.5 613.8 %all-gather.6.cloned.1.call-start = ((), (), s32[]{:S(2)}) async-start(), calls=%async_computation | async-start | bytes 9437184 | tf_op jit(solution)/shard_map/all_gather | solution.py:39
  51.4 811.7 %all-reduce.7.cloned.1.call-start = ((), (), s32[]{:S(2)}) async-start(), calls=%async_computation.6 | async-start | bytes 21626880 | tf_op jit(solution)/shard_map/psum | solution.py:55
  51.5 30.9 %copy-start.13 = (s32[512]{0:T(512)}, s32[512]{0:T(512)S(1)}, u32[]{:S(2)}) copy-start(s32[512]{0:T(512)S(1)} %iota_add_fusion) | copy-start | bytes 6148
  672.6 443.4 %all-reduce.5.cloned.1.call-start = ((), (), s32[]{:S(2)}) async-start(), calls=%async_computation.5 | async-start | bytes 21626880 | tf_op jit(solution)/shard_map/psum | solution.py:55
  887.0 5.0 slice-start.8
  891.7 8.1 slice-start
  893.8 6.0 slice-start.1
  893.8 6.0 copy-start.11
  893.8 11.9 slice-start.2
  899.8 5.9 slice-start.3
  899.9 5.9 copy-start.10
  899.9 11.7 slice-start.4
  905.7 5.9 slice-start.5
  905.7 5.9 copy-start.9
  905.8 11.9 %slice-start.6 = ((s8[8388608]{0:T(1024)(128)(4,1)}), s8[4194304]{0:T(1024)(128)(4,1)S(1)}, s32[]{:S(2)}) async-start(s8[8388608]{0:T(1024)(128)(4,1)} %bitcast.345), calls=%async_computation.13 | async-start | bytes 8388608
  911.6 6.1 slice-start.7
  911.6 6.1 copy-start.8
  1140.3 4.5 copy-start.26
  1140.3 4.5 copy-start.25
  1144.7 37.8 %copy-start.31 = (f32[6,8,512]{2,1,0:T(8,128)}, f32[6,8,512]{2,1,0:T(8,128)S(1)}, u32[]{:S(2)}) copy-start(f32[6,8,512]{2,1,0:T(8,128)S(1)} %constant_dynamic-update-slice_fusion.7) | copy-start | bytes 294916
  (25 other events, 81.6 us)
Sparse Core Ops, SparseCore 0:
  32.9 127.8 all-gather.7
  162.8 123.1 all-gather.9
  288.0 123.1 all-gather.11
  413.1 123.1 all-gather.13
  538.1 123.1 all-gather.5
  672.7 190.3 all-reduce.6
  923.7 192.3 all-reduce.4
where the time goes:
time: 1190 us
  waiting for transfers between devices  910 us (76%)
  matrix products  144 us (12%)
  blocking collectives  46.6 us (4%)
  other arithmetic  36.7 us (3%)
  between operations  27.8 us (2%)
  local copies, waits for them, and re-layouts  24.2 us (2%)
    all_gather x5, waiting for transfers between devices, body(): blocks[current_sup] = lax.all_gather(mine, 'col', axis=1, tiled=True)  530 us
    psum x2, waiting for transfers between devices, solve(): summed = lax.psum(jnp.concatenate([unit_part, rhs_part], axis=0), 'row')  380 us
    dot_general x31, matrix products, product(): jnp.dot(left, right, precision=HIGH, preferred_element_type=jnp.float32)  144 us
    psum x1, blocking collectives, body(): variance = lax.psum(jnp.stack(squares), 'col')  37.7 us
  transfers between devices with their start and end apart: 7, of which 7 were waited for; matrix products, arithmetic and copies ran while one was open for 7% of the time, Pallas kernels for 0%

commit v1 on v0

--- a/solution.py
+++ b/solution.py
@@ -52,7 +52,9 @@
     rhs = jnp.stack([product(gathered[s], lower[s]) for s in range(super_count)])
 
     def solve(current_sup, unit_part, rhs_part):
-        summed = lax.psum(jnp.concatenate([unit_part, rhs_part], axis=0), "row")
+        summed = jnp.sum(
+            lax.all_gather(jnp.concatenate([unit_part, rhs_part], axis=0), "row"), axis=0
+        )
         right = jnp.concatenate(
             [-summed[:col_width], gathered[current_sup] - summed[col_width:]], axis=0
         )

time: 1190 us -> 1400 us (1.18)
  waiting for transfers between devices: 910 us -> 1040 us
  other arithmetic: 36.7 us -> 93.1 us
  matrix products: 144 us -> 159 us
    all_gather x0 -> x10, waiting for transfers between devices: none -> 511 us  [solve(): lax.all_gather(jnp.concatenate([unit_part, rhs_part], axis=0), 'row')]
    psum x2 -> x0, waiting for transfers between devices: 380 us -> none  [solve(): summed = lax.psum(jnp.concatenate([unit_part, rhs_part], axis=0), 'row')]
    reduce_sum x0 -> x10, other arithmetic: none -> 56.5 us  [solve(): jnp.sum(lax.all_gather(jnp.concatenate([unit_part, rhs_part], axis=0), 'r...]
    dot_general x31, matrix products: 144 us -> 159 us  [product(): jnp.dot(left, right, precision=HIGH, preferred_element_type=jnp.float32)]
  transfers between devices with their start and end apart: 7 -> 15, of which waited for: 7 -> 15; matrix products, arithmetic and copies ran while one was open for 7% -> 13% of each run, Pallas kernels for 0% -> 0%
where the time goes in v1:
time: 1400 us; the launch traced here: 1390 us
  waiting for transfers between devices  1040 us (74%)
  matrix products  159 us (11%)
  other arithmetic  93.1 us (7%)
  blocking collectives  46.2 us (3%)
  between operations  27.1 us (2%)
  local copies, waits for them, and re-layouts  24.7 us (2%)
    all_gather x5, waiting for transfers between devices, body(): blocks[current_sup] = lax.all_gather(mine, 'col', axis=1, tiled=True)  530 us
    all_gather x10, waiting for transfers between devices, solve(): lax.all_gather(jnp.concatenate([unit_part, rhs_part], axis=0), 'row')  511 us
    dot_general x31, matrix products, product(): jnp.dot(left, right, precision=HIGH, preferred_element_type=jnp.float32)  159 us
    reduce_sum x10, other arithmetic, solve(): jnp.sum(lax.all_gather(jnp.concatenate([unit_part, rhs_part], axis=0), 'r...  56.5 us
    psum x1, blocking collectives, body(): variance = lax.psum(jnp.stack(squares), 'col')  37.7 us
  transfers between devices with their start and end apart: 15, of which 15 were waited for; matrix products, arithmetic and copies ran while one was open for 13% of the time, Pallas kernels for 0%

profile of v1, /device:TPU:0, one launch (start us, length us, event | category | flops | bytes accessed | tf_op | source)
XLA Modules:
  0.0 1392.8 jit_solution(14972160799708784)
XLA Ops:
  16.6 10.9 fusion.291
  50.5 8.5 all_gather.79
  83.6 76.4 %all-gather.34.cloned.1.call-done = f32[1024,2048]{1,0:T(8,128)} async-done(((f32[1024,256]{1,0:T(8,128)}), f32[1024,2048]{1,0:T(8,128)}) %all-gather.34.cloned.1.call-update) | async-done | bytes 8388624 | tf_op jit(solution)/shard_map/all_gather | solution.py:39
  171.7 113.5 %all-gather.32.cloned.1.call-done = f32[1024,2048]{1,0:T(8,128)} async-done(((f32[1024,256]{1,0:T(8,128)}), f32[1024,2048]{1,0:T(8,128)}) %all-gather.32.cloned.1.call-update) | async-done | bytes 8388624 | tf_op jit(solution)/shard_map/all_gather | solution.py:39
  296.7 113.7 %all-gather.30.cloned.1.call-done = f32[1024,2048]{1,0:T(8,128)} async-done(((f32[1024,256]{1,0:T(8,128)}), f32[1024,2048]{1,0:T(8,128)}) %all-gather.30.cloned.1.call-update) | async-done | bytes 8388624 | tf_op jit(solution)/shard_map/all_gather | solution.py:39
  422.3 113.1 %all-gather.28.cloned.1.call-done = f32[1024,2048]{1,0:T(8,128)} async-done(((f32[1024,256]{1,0:T(8,128)}), f32[1024,2048]{1,0:T(8,128)}) %all-gather.28.cloned.1.call-update) | async-done | bytes 8388624 | tf_op jit(solution)/shard_map/all_gather | solution.py:39
  547.0 113.5 %all-gather.26.cloned.1.call-done = f32[1024,2048]{1,0:T(8,128)} async-done(((f32[1024,256]{1,0:T(8,128)}), f32[1024,2048]{1,0:T(8,128)}) %all-gather.26.cloned.1.call-update) | async-done | bytes 8388624 | tf_op jit(solution)/shard_map/all_gather | solution.py:39
  664.7 6.5 fusion.200
  675.5 44.4 %all-gather.44.cloned.1.call-done = f32[1056,2048]{1,0:T(8,128)} async-done(((f32[264,2048]{1,0:T(8,128)}), f32[1056,2048]{1,0:T(8,128)}) %all-gather.44.cloned.1.call-update) | async-done | bytes 8650768 | tf_op jit(solution)/shard_map/all_gather | solution.py:56
  724.4 56.8 %all-gather.42.cloned.1.call-done = f32[1056,2048]{1,0:T(8,128)} async-done(((f32[264,2048]{1,0:T(8,128)}), f32[1056,2048]{1,0:T(8,128)}) %all-gather.42.cloned.1.call-update) | async-done | bytes 8650768 | tf_op jit(solution)/shard_map/all_gather | solution.py:56
  787.2 55.4 %all-gather.40.cloned.1.call-done = f32[1056,2048]{1,0:T(8,128)} async-done(((f32[264,2048]{1,0:T(8,128)}), f32[1056,2048]{1,0:T(8,128)}) %all-gather.40.cloned.1.call-update) | async-done | bytes 8650768 | tf_op jit(solution)/shard_map/all_gather | solution.py:56
  842.6 6.0 reduce_sum.236
  848.5 55.4 %all-gather.38.cloned.1.call-done = f32[1056,2048]{1,0:T(8,128)} async-done(((f32[264,2048]{1,0:T(8,128)}), f32[1056,2048]{1,0:T(8,128)}) %all-gather.38.cloned.1.call-update) | async-done | bytes 8650768 | tf_op jit(solution)/shard_map/all_gather | solution.py:56
  909.8 55.3 %all-gather.36.cloned.1.call-done = f32[1056,2048]{1,0:T(8,128)} async-done(((f32[264,2048]{1,0:T(8,128)}), f32[1056,2048]{1,0:T(8,128)}) %all-gather.36.cloned.1.call-update) | async-done | bytes 8650768 | tf_op jit(solution)/shard_map/all_gather | solution.py:56
  1009.0 9.0 fusion.163
  1018.1 10.4 fusion.155
  1028.6 9.0 fusion.147
  1037.8 9.2 fusion.139
  1047.3 21.2 %all-gather.54.cloned.1.call-done = f32[1056,2048]{1,0:T(8,128)} async-done(((f32[264,2048]{1,0:T(8,128)}), f32[1056,2048]{1,0:T(8,128)}) %all-gather.54.cloned.1.call-update) | async-done | bytes 8650768 | tf_op jit(solution)/shard_map/all_gather | solution.py:56
  1073.0 56.6 %all-gather.52.cloned.1.call-done = f32[1056,2048]{1,0:T(8,128)} async-done(((f32[264,2048]{1,0:T(8,128)}), f32[1056,2048]{1,0:T(8,128)}) %all-gather.52.cloned.1.call-update) | async-done | bytes 8650768 | tf_op jit(solution)/shard_map/all_gather | solution.py:56
  1135.6 55.4 %all-gather.50.cloned.1.call-done = f32[1056,2048]{1,0:T(8,128)} async-done(((f32[264,2048]{1,0:T(8,128)}), f32[1056,2048]{1,0:T(8,128)}) %all-gather.50.cloned.1.call-update) | async-done | bytes 8650768 | tf_op jit(solution)/shard_map/all_gather | solution.py:56
  1196.9 55.3 %all-gather.48.cloned.1.call-done = f32[1056,2048]{1,0:T(8,128)} async-done(((f32[264,2048]{1,0:T(8,128)}), f32[1056,2048]{1,0:T(8,128)}) %all-gather.48.cloned.1.call-update) | async-done | bytes 8650768 | tf_op jit(solution)/shard_map/all_gather | solution.py:56
  1258.1 55.3 %all-gather.46.cloned.1.call-done = f32[1056,2048]{1,0:T(8,128)} async-done(((f32[264,2048]{1,0:T(8,128)}), f32[1056,2048]{1,0:T(8,128)}) %all-gather.46.cloned.1.call-update) | async-done | bytes 8650768 | tf_op jit(solution)/shard_map/all_gather | solution.py:56
  1348.4 37.7 %psum.7 = f32[6,512]{1,0:T(8,128)} all-reduce(f32[6,512]{1,0:T(8,128)S(1)} %stack.112), channel_id=1, replica_groups=mesh['row'=4,'col'=8] {'col'}, use_global_device_ids=true, to_apply=%region_26.27 | all-reduce | flops 3072 | bytes 24576 | tf_op jit(solution)/shard_map/psum | solution.py:91
  (212 shorter events, 217.3 us)
Async XLA Ops:
  7.2 152.8 %all-gather.34.cloned.1.call-start = ((), (), s32[]{:S(2)}) async-start(), calls=%async_computation.4 | async-start | bytes 9437184 | tf_op jit(solution)/shard_map/all_gather | solution.py:39
  16.6 11.0 copy-start.19
  32.3 252.9 %all-gather.32.cloned.1.call-start = ((), (), s32[]{:S(2)}) async-start(), calls=%async_computation.3 | async-start | bytes 9437184 | tf_op jit(solution)/shard_map/all_gather | solution.py:39
  34.7 375.7 %all-gather.30.cloned.1.call-start = ((), (), s32[]{:S(2)}) async-start(), calls=%async_computation.2 | async-start | bytes 9437184 | tf_op jit(solution)/shard_map/all_gather | solution.py:39
  44.2 491.3 %all-gather.28.cloned.1.call-start = ((), (), s32[]{:S(2)}) async-start(), calls=%async_computation.1 | async-start | bytes 9437184 | tf_op jit(solution)/shard_map/all_gather | solution.py:39
  46.5 614.0 %all-gather.26.cloned.1.call-start = ((), (), s32[]{:S(2)}) async-start(), calls=%async_computation | async-start | bytes 9437184 | tf_op jit(solution)/shard_map/all_gather | solution.py:39
  50.5 669.4 %all-gather.44.cloned.1.call-start = ((), (), s32[]{:S(2)}) async-start(), calls=%async_computation.9 | async-start | bytes 10813440 | tf_op jit(solution)/shard_map/all_gather | solution.py:56
  50.5 30.6 %copy-start.7 = (s32[512]{0:T(512)}, s32[512]{0:T(512)S(1)}, u32[]{:S(2)}) copy-start(s32[512]{0:T(512)S(1)} %iota_add_fusion) | copy-start | bytes 6148
  171.7 609.5 %all-gather.42.cloned.1.call-start = ((), (), s32[]{:S(2)}) async-start(), calls=%async_computation.8 | async-start | bytes 10813440 | tf_op jit(solution)/shard_map/all_gather | solution.py:56
  296.7 545.9 %all-gather.40.cloned.1.call-start = ((), (), s32[]{:S(2)}) async-start(), calls=%async_computation.7 | async-start | bytes 10813440 | tf_op jit(solution)/shard_map/all_gather | solution.py:56
  421.9 482.0 %all-gather.38.cloned.1.call-start = ((), (), s32[]{:S(2)}) async-start(), calls=%async_computation.6 | async-start | bytes 10813440 | tf_op jit(solution)/shard_map/all_gather | solution.py:56
  547.0 418.1 %all-gather.36.cloned.1.call-start = ((), (), s32[]{:S(2)}) async-start(), calls=%async_computation.5 | async-start | bytes 10813440 | tf_op jit(solution)/shard_map/all_gather | solution.py:56
  672.7 395.7 %all-gather.54.cloned.1.call-start = ((), (), s32[]{:S(2)}) async-start(), calls=%async_computation.14 | async-start | bytes 10813440 | tf_op jit(solution)/shard_map/all_gather | solution.py:56
  995.1 6.1 slice-start
  1008.6 121.1 %all-gather.52.cloned.1.call-start = ((), (), s32[]{:S(2)}) async-start(), calls=%async_computation.13 | async-start | bytes 10813440 | tf_op jit(solution)/shard_map/all_gather | solution.py:56
  1018.1 173.0 %all-gather.50.cloned.1.call-start = ((), (), s32[]{:S(2)}) async-start(), calls=%async_computation.12 | async-start | bytes 10813440 | tf_op jit(solution)/shard_map/all_gather | solution.py:56
  1028.5 223.7 %all-gather.48.cloned.1.call-start = ((), (), s32[]{:S(2)}) async-start(), calls=%async_computation.11 | async-start | bytes 10813440 | tf_op jit(solution)/shard_map/all_gather | solution.py:56
  1037.6 275.8 %all-gather.46.cloned.1.call-start = ((), (), s32[]{:S(2)}) async-start(), calls=%async_computation.10 | async-start | bytes 10813440 | tf_op jit(solution)/shard_map/all_gather | solution.py:56
  1343.8 4.4 copy-start.24
  1343.8 4.5 copy-start.23
  1343.8 4.5 copy-start.22
  1343.8 4.5 copy-start.21
  1343.8 4.5 copy-start.20
  1348.2 37.8 %copy-start.26 = (f32[6,8,512]{2,1,0:T(8,128)}, f32[6,8,512]{2,1,0:T(8,128)S(1)}, u32[]{:S(2)}) copy-start(f32[6,8,512]{2,1,0:T(8,128)S(1)} %constant_dynamic-update-slice_fusion.7) | copy-start | bytes 294916
  (20 other events, 64.5 us)
Sparse Core Ops, SparseCore 0:
  32.4 127.5 all-gather.33
  162.0 123.1 all-gather.31
  287.2 123.1 all-gather.29
  412.3 123.1 all-gather.27
  537.3 123.1 all-gather.25
  661.9 57.9 all-gather.43
  721.4 59.7 all-gather.41
  782.8 59.7 all-gather.39
  844.1 59.7 all-gather.37
  905.3 59.7 all-gather.35
  1008.7 59.7 all-gather.53
  1069.9 59.7 all-gather.51
  1131.2 59.7 all-gather.49
  1192.4 59.7 all-gather.47
  1253.6 59.7 all-gather.45
